TPU v7x, 512 devices: a whole 4x8x8 slice. The times are simulated.
512 devices in a mesh: dp: 8 (over y), pipe: 4 (over z_lo), tensor: 16 (over z_hi, x, core).
Axes of the slice: x: 4, y: 8, z: 8 (z_hi: 2, z_lo: 4; z = z_hi * 4 + z_lo), core: 2. Of those that a mesh axis runs over, the one named last changes fastest.
Arguments:
- activations: bfloat16 [4, 1536, 4096], P('pipe', 'tensor', 'dp'), may hold values from -6 to 6
- upstream: bfloat16 [4, 1536, 4096], P('pipe', 'tensor', 'dp'), may hold values from -4 to 4
- gate_value: bfloat16 [4, 1536, 14336], P('pipe', 'dp', 'tensor'), may hold values from -6 to 6
- up_value: bfloat16 [4, 1536, 14336], P('pipe', 'dp', 'tensor'), may hold values from -6 to 6
- hidden_grad: bfloat16 [4, 1536, 14336], P('pipe', 'dp', 'tensor'), may hold values from -4 to 4
- gate_weight: bfloat16 [4, 4096, 14336], P('pipe', 'dp', 'tensor'), may hold values from -0.09375 to 0.09375
- up_weight: bfloat16 [4, 4096, 14336], P('pipe', 'dp', 'tensor'), may hold values from -0.09375 to 0.09375
- gate_mask: int32 [4, 32, 112], P('pipe', 'dp', 'tensor'), may hold values 0 or 1
- up_mask: int32 [4, 32, 112], P('pipe', 'dp', 'tensor'), may hold values 0 or 1
Outputs:
- gate_gradient: bfloat16 [4, 4096, 14336], P('pipe', 'dp', 'tensor')
- up_gradient: bfloat16 [4, 4096, 14336], P('pipe', 'dp', 'tensor')
- handed_back: bfloat16 [4, 1536, 4096], P('pipe', 'tensor', 'dp')
Inputs may be any that keep to these rules, and one draw needn't show every extreme that they name: gate_mask[s, i, j] keeps (1) or prunes (0) block (i, j) of gate_weight[s]. up_mask[s, i, j] keeps (1) or prunes (0) block (i, j) of up_weight[s].
All inputs are finite; a program needn't handle non-finite values.
Results may differ from a plain program's by a relative error of at most 0.0049.
Values may be sent and summed in bfloat16 or wider, within the bound.
A program may use at most 64 MiB of HBM per device.

v0:
```python
import jax
import jax.numpy as jnp
from jax import lax
from jax.sharding import PartitionSpec as P


def shifted(array, axis, by):
    devices = lax.axis_size(axis)
    pairs = [(i, i + by) for i in range(devices) if 0 <= i + by < devices]
    return lax.ppermute(array, axis, pairs)


def apply_blocks(matrix, keep_mask):
    rows_blocks, cols_blocks = keep_mask.shape
    shaped = matrix.reshape(
        rows_blocks, matrix.shape[0] // rows_blocks, cols_blocks, matrix.shape[1] // cols_blocks
    )
    return (shaped * keep_mask.astype(matrix.dtype)[:, None, :, None]).reshape(matrix.shape)


def per_device(
    activations,
    upstream,
    gate_value,
    up_value,
    hidden_grad,
    gate_weight,
    up_weight,
    gate_mask,
    up_mask,
):
    gathered = lax.all_gather(activations, "tensor", axis=1, tiled=True)[0]
    gate_float = gate_value[0].astype(jnp.float32)
    up_float = up_value[0].astype(jnp.float32)
    hidden_float = hidden_grad[0].astype(jnp.float32)
    gate_sigmoid = jax.nn.sigmoid(gate_float)
    up_delta = (hidden_float * gate_float * gate_sigmoid).astype(jnp.bfloat16)
    gate_delta = (
        hidden_float * up_float * gate_sigmoid * (1.0 + gate_float * (1.0 - gate_sigmoid))
    ).astype(jnp.bfloat16)
    gate_kept = apply_blocks(gate_weight[0], gate_mask[0])
    up_kept = apply_blocks(up_weight[0], up_mask[0])
    over_tokens = (((0,), (0,)), ((), ()))
    over_hidden = (((1,), (1,)), ((), ()))
    gate_piece = lax.all_gather(gate_delta, "dp", axis=0, tiled=True)
    up_piece = lax.all_gather(up_delta, "dp", axis=0, tiled=True)
    gate_acc = lax.dot_general(
        gathered, gate_piece, over_tokens, preferred_element_type=jnp.float32
    )
    up_acc = lax.dot_general(gathered, up_piece, over_tokens, preferred_element_type=jnp.float32)
    partial_rows = lax.dot_general(
        gate_piece, gate_kept, over_hidden, preferred_element_type=jnp.float32
    )
    partial_rows = partial_rows + lax.dot_general(
        up_piece, up_kept, over_hidden, preferred_element_type=jnp.float32
    )
    branch = partial_rows
    gate_acc, up_acc, branch = (gate_acc, up_acc, branch)
    own_rows = lax.psum_scatter(branch, "tensor", scatter_dimension=0, tiled=True)
    gate_gradient = apply_blocks(gate_acc, gate_mask[0]).astype(jnp.bfloat16)[None]
    up_gradient = apply_blocks(up_acc, up_mask[0]).astype(jnp.bfloat16)[None]
    section_grad = (upstream[0].astype(jnp.float32) + own_rows).astype(jnp.bfloat16)
    handed = shifted(section_grad, "pipe", -1)
    return (gate_gradient, up_gradient, handed[None])


def solution(mesh):
    return jax.shard_map(
        per_device,
        mesh=mesh,
        in_specs=(
            P("pipe", "tensor", "dp"),
            P("pipe", "tensor", "dp"),
            P("pipe", "dp", "tensor"),
            P("pipe", "dp", "tensor"),
            P("pipe", "dp", "tensor"),
            P("pipe", "dp", "tensor"),
            P("pipe", "dp", "tensor"),
            P("pipe", "dp", "tensor"),
            P("pipe", "dp", "tensor"),
        ),
        out_specs=(P("pipe", "dp", "tensor"), P("pipe", "dp", "tensor"), P("pipe", "tensor", "dp")),
        check_vma=False,
    )
```

profile of v0, /device:TPU:64, one launch (start us, length us, event | category | flops | bytes accessed | tf_op | source)
XLA Modules:
  0.0 296.9 jit_solution(10414191053938637605)
XLA Ops:
  7.2 0.0 copy-start
  7.2 0.0 copy-start.3
  7.2 0.0 copy-start.1
  7.2 0.0 all-gather.4.cloned.1.call-start
  7.2 2.5 fusion.29
  9.8 0.0 all-gather.4.cloned.1.call-update
  9.8 0.0 all-gather.8.cloned.1.call-start
  9.8 0.7 all-gather.8.cloned.1.call-update
  10.5 0.0 all-gather.6.cloned.1.call-start
  10.6 0.7 all-gather.6.cloned.1.call-update
  11.3 0.0 reduce-scatter.2.cloned.1.call-start
  11.3 0.8 convert_bitcast_fusion.3
  12.1 0.1 copy.19
  12.2 0.0 copy-done
  12.2 0.5 copy.18
  12.7 0.0 copy-done.3
  12.7 0.1 copy.21
  12.8 0.0 copy-done.1
  12.9 0.5 copy.20
  13.4 46.9 %all-gather.4.cloned.1.call-done = bf16[1536,896]{1,0:T(8,128)(2,1)} async-done(((bf16[192,896]{1,0:T(8,128)(2,1)}), bf16[1536,896]{1,0:T(8,128)(2,1)}) %all-gather.4.cloned.1.call-update) | async-done | bytes 2752528 | tf_op jit(solution)/shard_map/all_gather | solution.py:45
  60.3 0.3 mul.74
  60.6 5.3 %fusion.17 = f32[1536,512]{1,0:T(8,128)} fusion(bf16[1536,896]{1,0:T(8,128)(2,1)} %all-gather.4.cloned.1.call-done, bf16[112,8,4,128]{3,2,1,0:T(4,128)(2,1)S(1)} %bitcast.99, bf16[1,512,896]{1,2,0:T(8,128)(2,1)S(1)} %copy.18), kind=kOutput, calls=%fused_computation.17 | convolution fusion | flops 1409744896 | bytes 7733248 | tf_op jit(solution)/shard_map/dot_general | solution.py:51
  65.8 41.5 %all-gather.8.cloned.1.call-done = bf16[1536,896]{1,0:T(8,128)(2,1)} async-done(((bf16[192,896]{1,0:T(8,128)(2,1)}), bf16[1536,896]{1,0:T(8,128)(2,1)}) %all-gather.8.cloned.1.call-update) | async-done | bytes 2752528 | tf_op jit(solution)/shard_map/all_gather | solution.py:46
  107.3 0.3 mul.77
  107.6 6.2 %convolution_add_fusion = f32[1536,512]{1,0:T(8,128)} fusion(f32[1536,512]{1,0:T(8,128)} %fusion.17, bf16[1536,896]{1,0:T(8,128)(2,1)} %all-gather.8.cloned.1.call-done, bf16[112,8,4,128]{3,2,1,0:T(4,128)(2,1)S(1)} %bitcast.98, bf16[1,512,896]{1,2,0:T(8,128)(2,1)S(1)} %copy.20), kind=kOutput, calls=%fused_computation | convolution fusion | flops 1410531328 | bytes 10878976 | tf_op jit(solution)/shard_map/dot_general | solution.py:54
  113.8 0.0 reduce-scatter.2.cloned.1.call-update
  113.9 0.1 copy.16
  114.0 0.1 copy.17
  114.1 58.1 %all-gather.6.cloned.1.call-done = bf16[1,1536,512]{2,1,0:T(8,128)(2,1)} async-done(((bf16[1,96,512]{2,1,0:T(8,128)(2,1)}), bf16[1,1536,512]{2,1,0:T(8,128)(2,1)}) %all-gather.6.cloned.1.call-update) | async-done | bytes 1572880 | tf_op jit(solution)/shard_map/all_gather | solution.py:32
  172.2 0.3 mul.66
  172.5 0.0 copy-start.2
  172.5 3.9 %fusion.10 = bf16[1,512,896]{1,2,0:T(8,128)(2,1)S(1)} fusion(f32[112,8,4,128]{3,2,1,0:T(4,128)S(1)} %bitcast.97, bf16[1536,896]{1,0:T(8,128)(2,1)} %all-gather.4.cloned.1.call-done, bf16[1,1536,512]{2,1,0:T(8,128)(2,1)} %all-gather.6.cloned.1.call-done), kind=kOutput, calls=%fused_computation.9 | convolution fusion | flops 1410203648 | bytes 7077888 | tf_op jit(solution)/shard_map/dot_general | solution.py:47
  176.4 100.5 %reduce-scatter.2.cloned.1.call-done = f32[96,512]{1,0:T(8,128)} async-done(((f32[1536,512]{1,0:T(8,128)}), f32[96,512]{1,0:T(8,128)}) %reduce-scatter.2.cloned.1.call-update) | async-done | bytes 196624 | tf_op jit(solution)/shard_map/reduce_scatter | solution.py:59
  276.9 0.0 copy-done.2
  276.9 0.9 fusion.30
  277.9 5.2 %collective-permute-start = (bf16[96,512]{1,0:T(8,128)(2,1)S(1)}, bf16[96,512]{1,0:T(8,128)(2,1)S(1)}, u32[]{:S(2)}, u32[]{:S(2)}) collective-permute-start(bf16[96,512]{1,0:T(8,128)(2,1)S(1)} %fusion.30), channel_id=1, source_target_pairs={{16,0},{32,16},{48,32},{17,1},{33,17},{49,33},{18,2},{34,18},{50,3... | collective-permute-start | bytes 294920 | tf_op jit(solution)/shard_map/ppermute | solution.py:10
  283.1 0.3 mul.71
  283.4 3.8 %fusion.13 = bf16[1,512,896]{1,2,0:T(8,128)(2,1)S(1)} fusion(f32[112,8,4,128]{3,2,1,0:T(4,128)S(1)} %bitcast.96, bf16[1536,896]{1,0:T(8,128)(2,1)} %all-gather.8.cloned.1.call-done, bf16[1,1536,512]{2,1,0:T(8,128)(2,1)} %all-gather.6.cloned.1.call-done), kind=kOutput, calls=%fused_computation.10 | convolution fusion | flops 1410203648 | bytes 7077888 | tf_op jit(solution)/shard_map/dot_general | solution.py:50
  287.2 1.3 copy.22
  288.5 1.3 copy.23
  289.8 0.0 collective-permute-done
  289.8 0.6 copy.43
  (1 shorter events, 0.0 us)
Async XLA Ops:
  7.2 5.0 %copy-start = (bf16[1,512,896]{2,1,0:T(8,128)(2,1)S(1)}, bf16[1,512,896]{2,1,0:T(8,128)(2,1)}, u32[]{:S(2)}) copy-start(bf16[1,512,896]{2,1,0:T(8,128)(2,1)} %param.14) | copy-start | bytes 2752516
  7.2 5.5 %copy-start.3 = (s32[1,4,7]{2,1,0:T(4,128)S(1)}, s32[1,4,7]{2,1,0:T(4,128)}, u32[]{:S(2)}) copy-start(s32[1,4,7]{2,1,0:T(4,128)} %param.17) | copy-start | bytes 340
  7.2 5.7 %copy-start.1 = (bf16[1,512,896]{2,1,0:T(8,128)(2,1)S(1)}, bf16[1,512,896]{2,1,0:T(8,128)(2,1)}, u32[]{:S(2)}) copy-start(bf16[1,512,896]{2,1,0:T(8,128)(2,1)} %param.15) | copy-start | bytes 2752516
  7.2 53.1 %all-gather.4.cloned.1.call-start = ((), (), s32[]{:S(2)}) async-start(), calls=%async_computation.1 | async-start | bytes 3096576 | tf_op jit(solution)/shard_map/all_gather | solution.py:45
  9.8 97.5 %all-gather.8.cloned.1.call-start = ((), (), s32[]{:S(2)}) async-start(), calls=%async_computation.3 | async-start | bytes 3096576 | tf_op jit(solution)/shard_map/all_gather | solution.py:46
  10.5 161.7 %all-gather.6.cloned.1.call-start = ((), (), s32[]{:S(2)}) async-start(), calls=%async_computation.2 | async-start | bytes 1671168 | tf_op jit(solution)/shard_map/all_gather | solution.py:32
  11.3 265.7 %reduce-scatter.2.cloned.1.call-start = ((), (), s32[]{:S(2)}) async-start(), calls=%async_computation.4 | async-start | bytes 3342336 | tf_op jit(solution)/shard_map/reduce_scatter | solution.py:59
  172.5 104.4 %copy-start.2 = (bf16[1,96,512]{2,1,0:T(8,128)(2,1)S(1)}, bf16[1,96,512]{2,1,0:T(8,128)(2,1)}, u32[]{:S(2)}) copy-start(bf16[1,96,512]{2,1,0:T(8,128)(2,1)} %param.10) | copy-start | bytes 294916
  277.9 11.9 %collective-permute-start = (bf16[96,512]{1,0:T(8,128)(2,1)S(1)}, bf16[96,512]{1,0:T(8,128)(2,1)S(1)}, u32[]{:S(2)}, u32[]{:S(2)}) collective-permute-start(bf16[96,512]{1,0:T(8,128)(2,1)S(1)} %fusion.30), channel_id=1, source_target_pairs={{16,0},{32,16},{48,32},{17,1},{33,17},{49,33},{18,2},{34,18},{50,3... | collective-permute-start | bytes 294920 | tf_op jit(solution)/shard_map/ppermute | solution.py:10
Sparse Core Ops, SparseCore 0:
  10.7 49.5 all-gather.3
  62.9 44.3 all-gather.7
  110.6 61.5 all-gather.5
  176.9 99.9 reduce-scatter.1
where the time goes:
time: 297 us
  waiting for transfers between devices  248 us (84%)
  matrix products  19.2 us (6%)
  between operations  13.9 us (5%)
  local copies, waits for them, and re-layouts  5.86 us (2%)
  starting transfers between devices  5.31 us (2%)
  other arithmetic  4.23 us (1%)
    reduce_scatter x1, waiting for transfers between devices, per_device(): lax.psum_scatter(branch, 'tensor', scatter_dimension=0, tiled=True)  101 us
    all_gather x1, waiting for transfers between devices, per_device(): gathered = lax.all_gather(activations, 'tensor', axis=1, tiled=True)[0]  58.1 us
    all_gather x1, waiting for transfers between devices, per_device(): gate_piece = lax.all_gather(gate_delta, 'dp', axis=0, tiled=True)  46.9 us
    all_gather x1, waiting for transfers between devices, per_device(): up_piece = lax.all_gather(up_delta, 'dp', axis=0, tiled=True)  41.5 us
    dot_general x1, matrix products, per_device(): lax.dot_general(up_piece, up_kept, over_hidden, preferred_element_type=jn...  6.21 us
  transfers between devices with their start and end apart: 5, of which 4 were waited for; matrix products, arithmetic and copies ran while one was open for 8% of the time, Pallas kernels for 0%

commit v1 on v0

--- a/solution.py
+++ b/solution.py
@@ -2,6 +2,13 @@
 import jax.numpy as jnp
 from jax import lax
 from jax.sharding import PartitionSpec as P
+
+
+def cells_touch(array_here):
+    state_next = jnp.stack(lax.axis_size("dp") * [array_here], axis=0)
+    y = lax.all_to_all(state_next, axis_name="dp", split_axis=0, concat_axis=0)
+    even = jnp.concatenate(y, axis=0)
+    return even
 
 
 def shifted(array, axis, by):
@@ -42,7 +49,7 @@
     up_kept = apply_blocks(up_weight[0], up_mask[0])
     over_tokens = (((0,), (0,)), ((), ()))
     over_hidden = (((1,), (1,)), ((), ()))
-    gate_piece = lax.all_gather(gate_delta, "dp", axis=0, tiled=True)
+    gate_piece = cells_touch(gate_delta)
     up_piece = lax.all_gather(up_delta, "dp", axis=0, tiled=True)
     gate_acc = lax.dot_general(
         gathered, gate_piece, over_tokens, preferred_element_type=jnp.float32

time: 297 us -> 301 us (1.013)
  starting transfers between devices: 5.31 us -> 12.5 us
  waiting for transfers between devices: 248 us -> 242 us
  local copies, waits for them, and re-layouts: 5.86 us -> 9.79 us
    all_to_all x0 -> x1, waiting for transfers between devices: none -> 85.8 us  [cells_touch(): y = lax.all_to_all(state_next, axis_name='dp', split_axis=0, concat_axis=0)]
    all_gather x1 -> x0, waiting for transfers between devices: 46.9 us -> none  [per_device(): gate_piece = lax.all_gather(gate_delta, 'dp', axis=0, tiled=True)]
    all_gather x1, waiting for transfers between devices: 41.5 us -> 0.01 us  [per_device(): up_piece = lax.all_gather(up_delta, 'dp', axis=0, tiled=True)]
    all_to_all x0 -> x1, starting transfers between devices: none -> 7.23 us  [cells_touch(): y = lax.all_to_all(state_next, axis_name='dp', split_axis=0, concat_axis=0)]
    all_gather x1, waiting for transfers between devices: 58.1 us -> 54.7 us  [per_device(): gathered = lax.all_gather(activations, 'tensor', axis=1, tiled=True)[0]]
  transfers between devices with their start and end apart: 5 -> 5, of which waited for: 4 -> 3; matrix products, arithmetic and copies ran while one was open for 8% -> 9% of each run, Pallas kernels for 0% -> 0%
where the time goes in v1:
time: 301 us
  waiting for transfers between devices  242 us (80%)
  matrix products  19.4 us (6%)
  between operations  13.9 us (5%)
  starting transfers between devices  12.5 us (4%)
  local copies, waits for them, and re-layouts  9.79 us (3%)
  other arithmetic  3.27 us (1%)
    reduce_scatter x1, waiting for transfers between devices, per_device(): lax.psum_scatter(branch, 'tensor', scatter_dimension=0, tiled=True)  101 us
    all_to_all x1, waiting for transfers between devices, cells_touch(): y = lax.all_to_all(state_next, axis_name='dp', split_axis=0, concat_axis=0)  85.8 us
    all_gather x1, waiting for transfers between devices, per_device(): gathered = lax.all_gather(activations, 'tensor', axis=1, tiled=True)[0]  54.7 us
    all_to_all x1, starting transfers between devices, cells_touch(): y = lax.all_to_all(state_next, axis_name='dp', split_axis=0, concat_axis=0)  7.23 us
    dot_general x1, matrix products, per_device(): lax.dot_general(up_piece, up_kept, over_hidden, preferred_element_type=jn...  6.2 us
  transfers between devices with their start and end apart: 5, of which 3 were waited for; matrix products, arithmetic and copies ran while one was open for 9% of the time, Pallas kernels for 0%

profile of v1, /device:TPU:64, one launch (start us, length us, event | category | flops | bytes accessed | tf_op | source)
XLA Modules:
  0.0 300.8 jit_solution(2910156814967458798)
XLA Ops:
  7.2 0.0 all-gather.6.cloned.1.call-start
  7.2 2.3 fusion.35
  9.5 0.0 all-gather.6.cloned.1.call-update
  9.5 1.9 stack.5
  11.4 0.0 copy-start.4
  11.4 7.2 %all-to-all-start = ((bf16[8,192,896]{2,1,0:T(8,128)(2,1)}), bf16[8,192,896]{2,1,0:T(8,128)(2,1)}, u32[]{:S(2)}, u32[]{:S(2)}) async-start(bf16[8,192,896]{2,1,0:T(8,128)(2,1)} %stack.5), calls=%async_computation | async-start | bytes 5505024 | tf_op jit(solution)/shard_map/all_to_all | solution.py:9
  18.7 0.0 copy-start
  18.7 0.0 copy-start.5
  18.7 0.0 copy-start.1
  18.7 0.0 all-gather.4.cloned.1.call-start
  18.8 0.7 all-gather.4.cloned.1.call-update
  19.5 0.0 reduce-scatter.2.cloned.1.call-start
  19.5 0.0 copy-done.4
  19.5 0.1 copy.18
  19.6 0.3 mul.85
  19.9 1.3 mul.86
  21.2 0.0 copy-done
  21.2 0.0 copy-start.2
  21.2 1.3 copy.19
  22.5 0.0 copy-done.5
  22.5 0.1 copy.21
  22.6 0.0 copy-done.1
  22.6 0.5 copy.20
  23.2 85.8 %all-to-all-done = bf16[8,192,896]{2,1,0:T(8,128)(2,1)} async-done(((bf16[8,192,896]{2,1,0:T(8,128)(2,1)}), bf16[8,192,896]{2,1,0:T(8,128)(2,1)}, u32[]{:S(2)}, u32[]{:S(2)}) %all-to-all-start) | async-done | bytes 2752544 | tf_op jit(solution)/shard_map/all_to_all | solution.py:9
  109.0 0.0 copy-done.2
  109.0 5.5 %fusion.24 = f32[1536,512]{1,0:T(8,128)} fusion(bf16[1536,896]{1,0:T(8,128)(2,1)} %bitcast.1, bf16[1,512,896]{1,2,0:T(8,128)(2,1)} %copy.19, bf16[1,512,896]{1,2,0:T(8,128)(2,1)S(1)} %copy-done.2), kind=kOutput, calls=%fused_computation.19 | convolution fusion | flops 1409744896 | bytes 7733248 | tf_op jit(solution)/shard_map/dot_general | solution.py:58
  114.5 0.0 all-gather.6.cloned.1.call-done
  114.5 0.3 mul.89
  114.8 6.2 %convolution_add_fusion = f32[1536,512]{1,0:T(8,128)} fusion(f32[1536,512]{1,0:T(8,128)} %fusion.24, bf16[1,1536,896]{2,1,0:T(8,128)(2,1)} %all-gather.6.cloned.1.call-done, bf16[112,8,4,128]{3,2,1,0:T(4,128)(2,1)S(1)} %bitcast.90, bf16[1,512,896]{1,2,0:T(8,128)(2,1)S(1)} %copy.20), kind=kOutput, calls=%fused_computation | convolution fusion | flops 1410531328 | bytes 10878976 | tf_op jit(solution)/shard_map/dot_general | solution.py:61
  121.0 0.0 reduce-scatter.2.cloned.1.call-update
  121.0 0.1 copy.16
  121.1 0.1 copy.17
  121.2 54.7 %all-gather.4.cloned.1.call-done = bf16[1,1536,512]{2,1,0:T(8,128)(2,1)} async-done(((bf16[1,96,512]{2,1,0:T(8,128)(2,1)}), bf16[1,1536,512]{2,1,0:T(8,128)(2,1)}) %all-gather.4.cloned.1.call-update) | async-done | bytes 1572880 | tf_op jit(solution)/shard_map/all_gather | solution.py:39
  175.9 0.3 mul.76
  176.2 0.0 copy-start.3
  176.2 3.9 %fusion.14 = bf16[1,512,896]{1,2,0:T(8,128)(2,1)S(1)} fusion(f32[112,8,4,128]{3,2,1,0:T(4,128)S(1)} %bitcast.89, bf16[1536,896]{1,0:T(8,128)(2,1)} %bitcast.1, bf16[1,1536,512]{2,1,0:T(8,128)(2,1)} %all-gather.4.cloned.1.call-done), kind=kOutput, calls=%fused_computation.11 | convolution fusion | flops 1410203648 | bytes 7077888 | tf_op jit(solution)/shard_map/dot_general | solution.py:54
  180.1 100.7 %reduce-scatter.2.cloned.1.call-done = f32[96,512]{1,0:T(8,128)} async-done(((f32[1536,512]{1,0:T(8,128)}), f32[96,512]{1,0:T(8,128)}) %reduce-scatter.2.cloned.1.call-update) | async-done | bytes 196624 | tf_op jit(solution)/shard_map/reduce_scatter | solution.py:66
  280.8 0.0 copy-done.3
  280.8 0.9 fusion.37
  281.7 5.2 %collective-permute-start = (bf16[96,512]{1,0:T(8,128)(2,1)S(1)}, bf16[96,512]{1,0:T(8,128)(2,1)S(1)}, u32[]{:S(2)}, u32[]{:S(2)}) collective-permute-start(bf16[96,512]{1,0:T(8,128)(2,1)S(1)} %fusion.37), channel_id=1, source_target_pairs={{16,0},{32,16},{48,32},{17,1},{33,17},{49,33},{18,2},{34,18},{50,3... | collective-permute-start | bytes 294920 | tf_op jit(solution)/shard_map/ppermute | solution.py:17
  286.9 0.3 mul.82
  287.2 3.9 %fusion.17 = bf16[1,512,896]{1,2,0:T(8,128)(2,1)S(1)} fusion(f32[112,8,4,128]{3,2,1,0:T(4,128)S(1)} %bitcast.88, bf16[1,1536,512]{2,1,0:T(8,128)(2,1)} %all-gather.4.cloned.1.call-done, bf16[1,1536,896]{2,1,0:T(8,128)(2,1)} %all-gather.6.cloned.1.call-done), kind=kOutput, calls=%fused_computation.12 | convolution fusion | flops 1410203648 | bytes 7077888 | tf_op jit(solution)/shard_map/dot_general | solution.py:57
  291.1 1.3 copy.22
  292.4 1.3 copy.23
  293.6 0.0 collective-permute-done
  293.6 0.6 copy.38
  (2 shorter events, 0.0 us)
Async XLA Ops:
  7.2 107.3 %all-gather.6.cloned.1.call-start = ((), (), s32[]{:S(2)}) async-start(), calls=%async_computation.4 | async-start | bytes 3096576 | tf_op jit(solution)/shard_map/all_gather | solution.py:53
  11.4 8.1 %copy-start.4 = (s32[1,4,7]{2,1,0:T(4,128)S(1)}, s32[1,4,7]{2,1,0:T(4,128)}, u32[]{:S(2)}) copy-start(s32[1,4,7]{2,1,0:T(4,128)} %param.16) | copy-start | bytes 340
  11.4 97.5 %all-to-all-start = ((bf16[8,192,896]{2,1,0:T(8,128)(2,1)}), bf16[8,192,896]{2,1,0:T(8,128)(2,1)}, u32[]{:S(2)}, u32[]{:S(2)}) async-start(bf16[8,192,896]{2,1,0:T(8,128)(2,1)} %stack.5), calls=%async_computation | async-start | bytes 5505024 | tf_op jit(solution)/shard_map/all_to_all | solution.py:9
  18.7 2.5 copy-start
  18.7 3.8 %copy-start.5 = (s32[1,4,7]{2,1,0:T(4,128)S(1)}, s32[1,4,7]{2,1,0:T(4,128)}, u32[]{:S(2)}) copy-start(s32[1,4,7]{2,1,0:T(4,128)} %param.17) | copy-start | bytes 340
  18.7 3.9 %copy-start.1 = (bf16[1,512,896]{2,1,0:T(8,128)(2,1)S(1)}, bf16[1,512,896]{2,1,0:T(8,128)(2,1)}, u32[]{:S(2)}) copy-start(bf16[1,512,896]{2,1,0:T(8,128)(2,1)} %param.15) | copy-start | bytes 2752516
  18.7 157.2 %all-gather.4.cloned.1.call-start = ((), (), s32[]{:S(2)}) async-start(), calls=%async_computation.2 | async-start | bytes 1671168 | tf_op jit(solution)/shard_map/all_gather | solution.py:39
  19.5 261.3 %reduce-scatter.2.cloned.1.call-start = ((), (), s32[]{:S(2)}) async-start(), calls=%async_computation.3 | async-start | bytes 3342336 | tf_op jit(solution)/shard_map/reduce_scatter | solution.py:66
  21.2 87.8 %copy-start.2 = (bf16[1,512,896]{1,2,0:T(8,128)(2,1)S(1)}, bf16[1,512,896]{1,2,0:T(8,128)(2,1)}, u32[]{:S(2)}) copy-start(bf16[1,512,896]{1,2,0:T(8,128)(2,1)} %mul.86) | copy-start | bytes 2752516
  176.2 104.6 %copy-start.3 = (bf16[1,96,512]{2,1,0:T(8,128)(2,1)S(1)}, bf16[1,96,512]{2,1,0:T(8,128)(2,1)}, u32[]{:S(2)}) copy-start(bf16[1,96,512]{2,1,0:T(8,128)(2,1)} %param.10) | copy-start | bytes 294916
  281.7 11.9 %collective-permute-start = (bf16[96,512]{1,0:T(8,128)(2,1)S(1)}, bf16[96,512]{1,0:T(8,128)(2,1)S(1)}, u32[]{:S(2)}, u32[]{:S(2)}) collective-permute-start(bf16[96,512]{1,0:T(8,128)(2,1)S(1)} %fusion.37), channel_id=1, source_target_pairs={{16,0},{32,16},{48,32},{17,1},{33,17},{49,33},{18,2},{34,18},{50,3... | collective-permute-start | bytes 294920 | tf_op jit(solution)/shard_map/ppermute | solution.py:17
Sparse Core Ops, SparseCore 0:
  10.1 96.2 all-gather.5
  109.7 66.1 all-gather.3
  180.8 99.9 reduce-scatter.1
